TPU v7x, 128 devices: a whole 4x4x4 slice. The times are simulated.
128 devices in a mesh: lev: 64 (over z, x_hi, y, core), var: 2 (over x_lo).
Axes of the slice: x: 4 (x_hi: 2, x_lo: 2; x = x_hi * 2 + x_lo), y: 4, z: 4, core: 2. Of those that a mesh axis runs over, the one named last changes fastest.
Arguments:
- background: float32 [128, 4, 128, 1024], P('lev', 'var'), may hold values from -6 to 6
- field_ids: int32 [128, 1024], replicated, may hold values from 0 to 7
- filter_table: float32 [8, 128, 4, 2], P(None, 'lev', 'var'), may hold values from 0.02 to 0.24
- first_weight: bfloat16 [512, 1024], replicated, may hold values from -0.25 to 0.25
- first_bias: float32 [1024], replicated, may hold values from -3 to 3
- second_weight: bfloat16 [1024, 512], replicated, may hold values from -0.1875 to 0.1875
- second_bias: float32 [512], replicated, may hold values from -4 to 4
- predictor_index: int32 [512, 8], replicated, may hold values from 0 to 511
- predictor_coef: float32 [512, 8], replicated, may hold values from -3 to 3
- channel_level: int32 [512], replicated, may hold values from 0 to 127
- observed: float32 [128, 1024, 512], P(('lev', 'var')), may hold values from -10 to 10
Outputs:
- radiances: bfloat16 [128, 1024, 512], P(('lev', 'var'))
- mean_cost: float32 [], replicated
- gradient: float32 [128, 4, 128, 1024], P('lev', 'var')
All inputs are finite; a program needn't handle non-finite values.
Results may differ from a plain program's by a relative error of at most 0.005.
Values may be sent and summed in bfloat16 or wider, within the bound.
A program may use at most 128 MiB of HBM per device.

v0:
```python
import functools

import jax
import jax.numpy as jnp
from jax import lax
from jax.experimental import pallas as pl
from jax.experimental.pallas import tpu as pltpu
from jax.sharding import PartitionSpec as P

PASSES = 4
DEVICES = 128
PLANES = 4
LAT, LON = 128, 1024
STEP = 16
LANES = 128
STRIPS = 1024 // LANES
NQ = 4
CHUNKS = LON // (LANES * NQ)
ROWS = PLANES * NQ
COLS = LANES * NQ
FEATURES, UNITS, CHANNELS = 512, 1024, 512
MESH = pl.DeviceIdType.MESH
F32, BF16 = jnp.float32, jnp.bfloat16


def offset_of(number):
    return (number // 32, (number // 8) % 4, (number // 2) % 4, number % 2)


def hops_of(number):
    return sum(min(part, 4 - part) for part in offset_of(number)[:3])


ORDER = sorted(range(1, DEVICES), key=lambda n: (-hops_of(n), (n * 73 + 19) * 2654435761 % 4294967291))


def targets():
    lev, var = lax.axis_index("lev"), lax.axis_index("var")
    z, high, y, core = lev // 16, (lev // 8) % 2, (lev // 2) % 4, lev % 2
    x = high * 2 + var
    zs = [((z + d) % 4) * 16 for d in range(4)]
    ys = [((y + d) % 4) * 2 for d in range(4)]
    xs = [(x + d) % 4 for d in range(4)]
    cores = [(core + d) % 2 for d in range(2)]
    zy = [[a + b for b in ys] for a in zs]
    xc = [[(a // 2) * 8 + b for b in cores] for a in xs]
    low = [a % 2 for a in xs]
    found = []
    for number in ORDER:
        dz, dy, dx, dc = offset_of(number)
        found.append((zy[dz][dy] + xc[dx][dc], low[dx]))
    return lev * 2 + var, found


def scatter_rows(where, start, step, values):
    where[pl.ds(start, 8, stride=step), :] = values


def gather_rows(strips, k):
    return jnp.concatenate([strip[pl.ds(k, 8, stride=STEP), :] for strip in strips], axis=1)


def neighbours(held, k):
    sub = lax.broadcasted_iota(jnp.int32, (8, LON), 0)
    if k < STEP - 1:
        above = held[k + 1]
    else:
        above = jnp.where(sub == 7, 0.0, pltpu.roll(held[0], 7, 0))
    if k > 0:
        below = held[k - 1]
    else:
        below = jnp.where(sub == 0, 0.0, pltpu.roll(held[STEP - 1], 1, 0))
    return above, below


def sideways(value):
    return pltpu.roll(value, 1, 1) + pltpu.roll(value, LON - 1, 1)


def forward_kernel(
    grid_ref, ids_ref, table_ref, w1_ref, b1_ref, w2_ref, b2_ref, index_ref, coef_ref, level_ref, seen_ref,
    back_ref, lat_ref, lon_ref, rad_ref, cost_ref,
    planes, ids, flip, mixed, send, got, send_back, w1raw, w1, w2, obs, wide, sel_hi, sel_lo, turned,
    active_ref, total,
    grid_sem, ids_sem, w1_sem, w2_sem, obs_sem, own_sem, out1, in1, out2, in2, out3, in3,
):
    me, peers = targets()
    barrier = pltpu.get_barrier_semaphore()
    for lev, var in peers:
        pl.semaphore_signal(barrier, 1, device_id=(lev, var), device_id_type=MESH)
    strips = [pl.ds(j * LANES, LANES) for j in range(STRIPS)]
    ids_copies = [pltpu.make_async_copy(ids_ref.at[:, s], ids.at[j], ids_sem.at[j]) for j, s in enumerate(strips)]
    for copy in ids_copies:
        copy.start()
    grid_copies = [
        pltpu.make_async_copy(grid_ref.at[p, :, s], planes.at[p, j], grid_sem.at[p, j])
        for p in range(PLANES)
        for j, s in enumerate(strips)
    ]
    for copy in grid_copies:
        copy.start()
    w1_copy = pltpu.make_async_copy(w1_ref, w1raw, w1_sem)
    w2_copy = pltpu.make_async_copy(w2_ref, w2, w2_sem)
    obs_copy = pltpu.make_async_copy(seen_ref, obs, obs_sem)
    w1_copy.start()
    w2_copy.start()
    obs_copy.start()

    for copy in ids_copies:
        copy.wait()

    @pl.loop(0, STEP)
    def _(k):
        field = gather_rows([ids.at[j] for j in range(STRIPS)], k)
        bits = [(field & (1 << n)) != 0 for n in range(3)]
        for p in range(PLANES):
            for axis, where in ((0, lat_ref), (1, lon_ref)):
                level = [table_ref[n * 8 + p * 2 + axis] for n in range(8)]
                for bit in bits:
                    level = [jnp.where(bit, level[2 * n + 1], level[2 * n]) for n in range(len(level) // 2)]
                where[p, k] = level[0]

    for copy in grid_copies:
        copy.wait()

    @pl.loop(0, PLANES)
    def _(p):
        for k in range(STEP):
            flip[0, k] = gather_rows([planes.at[p, j] for j in range(STRIPS)], k)
        for number in range(PASSES):
            held = flip.at[number % 2]
            for k in range(STEP):
                above, below = neighbours(held, k)
                value = held[k]
                twice = value + value
                value = (
                    value
                    + lat_ref[p, k] * (above + below - twice)
                    + lon_ref[p, k] * (sideways(value) - twice)
                )
                if number < PASSES - 1:
                    flip[1 - number % 2, k] = value
                else:
                    for c in range(CHUNKS):
                        for q in range(NQ):
                            at = (c * NQ + q) * LANES
                            scatter_rows(
                                mixed.at[c], k * ROWS + p * NQ + q, STEP * ROWS, value[:, at : at + LANES]
                            )

    @pl.loop(0, CHUNKS)
    def _(c):
        @pl.loop(0, DEVICES, unroll=4)
        def _(d):
            send[c, d] = mixed[c, pl.ds(pl.multiple_of(d * ROWS, ROWS), ROWS), :].astype(BF16)

    pl.semaphore_wait(barrier, DEVICES - 1)

    @pl.loop(0, CHUNKS)
    def _(c):
        for lev, var in peers:
            pltpu.make_async_remote_copy(
                send.at[c, lev * 2 + var], got.at[c, me], out1.at[c], in1.at[c],
                device_id=(lev, var), device_id_type=MESH,
            ).start()
        pltpu.make_async_copy(send.at[c, me], got.at[c, me], own_sem.at[c]).start()

    row = lax.broadcasted_iota(jnp.int32, (CHANNELS, FEATURES), 1)
    feature = (row % 64) * 8 + (row // 256) * 4 + ((row // 64) % 2) * 2 + (row // 128) % 2
    picks = jnp.where(feature // 4 == level_ref[...], 1.0, 0.0).astype(F32)
    for n in range(8):
        picks = picks + jnp.where(feature == index_ref[:, n : n + 1], coef_ref[:, n : n + 1], 0.0)
    wide[0:FEATURES, 0:CHANNELS] = picks.T
    picks = wide[0:FEATURES, 0:CHANNELS]
    high = picks.astype(BF16)
    sel_hi[...] = high
    sel_lo[...] = (picks - high.astype(F32)).astype(BF16)
    w1_copy.wait()
    for part in range(UNITS // LANES):
        turned[0:FEATURES, :] = w1raw[:, part * LANES : (part + 1) * LANES].astype(F32)
        for s in range(8):
            block = turned[pl.ds(s, 64, stride=8), :]
            at = ((s // 4) * 2 + s % 2) * LANES + ((s // 2) % 2) * 64
            w1[at : at + 64, part * LANES : (part + 1) * LANES] = block.astype(BF16)
    w2_copy.wait()
    obs_copy.wait()
    total[...] = jnp.zeros_like(total)

    @pl.loop(0, CHUNKS)
    def _(c):
        pltpu.make_async_copy(send.at[c, me], got.at[c, me], own_sem.at[c]).wait()
        others = pl.ds(0, DEVICES - 1)
        pltpu.make_async_copy(got.at[c, others], got.at[c, others], in1.at[c]).wait()

        @pl.loop(0, DEVICES, unroll=4)
        def _(d):
            mixed[c, pl.ds(pl.multiple_of(d * ROWS, ROWS), ROWS), :] = got[c, d].astype(F32)

        for q in range(NQ):
            for p in range(PLANES):
                for var in range(2):
                    block = mixed[c, pl.ds(var * ROWS + p * NQ + q, 64, stride=2 * ROWS), :]
                    turned[p * LANES + var * 64 : p * LANES + var * 64 + 64, :] = block
            columns = turned[...].T.astype(BF16)
            first = pl.multiple_of(c * COLS + q * LANES, LANES)
            spot = pl.ds(first, LANES)
            active = jnp.tanh(jnp.dot(columns, w1[...], preferred_element_type=F32) + b1_ref[...])
            evolved = jnp.dot(active.astype(BF16), w2[...], preferred_element_type=F32) + b2_ref[...]
            evolved = evolved + jnp.dot(columns, sel_hi[...], preferred_element_type=F32)
            evolved = evolved + jnp.dot(columns, sel_lo[...], preferred_element_type=F32)
            rad_ref[spot, :] = evolved.astype(BF16)
            depart = evolved - obs[spot, :]
            total[...] += jnp.sum((depart * depart).reshape(LANES // 8, 8, CHANNELS), axis=0)
            depart_hi = depart.astype(BF16)
            depart_lo = (depart - depart_hi.astype(F32)).astype(BF16)
            turn = (((1,), (1,)), ((), ()))
            pull = lax.dot_general(depart_hi, w2[...], turn, preferred_element_type=F32)
            pull = (pull * (1.0 - active * active)).astype(BF16)
            slope = lax.dot_general(w1[...], pull, turn, preferred_element_type=F32)
            slope = slope + lax.dot_general(sel_hi[...], depart_hi, turn, preferred_element_type=F32)
            slope = slope + lax.dot_general(sel_lo[...], depart_hi, turn, preferred_element_type=F32)
            slope = slope + lax.dot_general(sel_hi[...], depart_lo, turn, preferred_element_type=F32)
            for p in range(PLANES):
                for var in range(2):
                    at = p * LANES + var * 64
                    mixed[c, pl.ds(var * ROWS + p * NQ + q, 64, stride=2 * ROWS), :] = slope[at : at + 64]

        @pl.loop(0, DEVICES, unroll=4)
        def _(d):
            send_back[c, d] = mixed[c, pl.ds(pl.multiple_of(d * ROWS, ROWS), ROWS), :].astype(BF16)

        for lev, var in peers:
            pltpu.make_async_remote_copy(
                send_back.at[c, lev * 2 + var], back_ref.at[c, me], out2.at[c], in2.at[c],
                device_id=(lev, var), device_id_type=MESH,
            ).start()
        pltpu.make_async_copy(send_back.at[c, me], back_ref.at[c, me], own_sem.at[c]).start()

    summed = jnp.sum(total[...], axis=0, keepdims=True)
    summed = sum(summed[:, n * LANES : (n + 1) * LANES] for n in range(CHANNELS // LANES))
    cost_ref[me] = summed
    for lev, var in peers:
        pltpu.make_async_remote_copy(
            cost_ref.at[me], cost_ref.at[me], out3, in3, device_id=(lev, var), device_id_type=MESH
        ).start()
    others = pl.ds(0, DEVICES - 1)
    for c in range(CHUNKS):
        pltpu.make_async_copy(send.at[c, others], send.at[c, others], out1.at[c]).wait()
        pltpu.make_async_copy(send_back.at[c, me], back_ref.at[c, me], own_sem.at[c]).wait()
        pltpu.make_async_copy(send_back.at[c, others], send_back.at[c, others], out2.at[c]).wait()
        pltpu.make_async_copy(back_ref.at[c, others], back_ref.at[c, others], in2.at[c]).wait()
    pltpu.make_async_copy(cost_ref.at[others], cost_ref.at[others], out3).wait()
    pltpu.make_async_copy(cost_ref.at[others], cost_ref.at[others], in3).wait()


def adjoint_kernel(
    back_ref, lat_ref, lon_ref, rad_ref, cost_ref,
    grad_ref, rad_out, mean_ref,
    mixed, flip, staged, rad_sem, grad_sem,
):
    rad_copy = pltpu.make_async_copy(rad_ref, rad_out, rad_sem)
    rad_copy.start()

    def leaving(p, j):
        strip = pl.ds(j * LANES, LANES)
        return pltpu.make_async_copy(staged.at[p, j], grad_ref.at[p, :, strip], grad_sem.at[p, j])

    for c in range(CHUNKS):

        @pl.loop(0, DEVICES, unroll=4)
        def _(d):
            mixed[c, pl.ds(pl.multiple_of(d * ROWS, ROWS), ROWS), :] = back_ref[c, d].astype(F32)

    @pl.loop(0, PLANES)
    def _(p):
        for k in range(STEP):
            pieces = [
                mixed[c, pl.ds(k * ROWS + p * NQ + q, 8, stride=STEP * ROWS), :]
                for c in range(CHUNKS)
                for q in range(NQ)
            ]
            flip[0, k] = jnp.concatenate(pieces, axis=1)
        for number in range(PASSES):
            held = flip.at[number % 2]
            sub = lax.broadcasted_iota(jnp.int32, (8, LON), 0)
            first = lat_ref[p, 0] * held[0]
            last = lat_ref[p, STEP - 1] * held[STEP - 1]
            below = jnp.where(sub == 0, 0.0, pltpu.roll(last, 1, 0))
            here = first
            for k in range(STEP):
                if k < STEP - 1:
                    above = lat_ref[p, k + 1] * held[k + 1]
                else:
                    above = jnp.where(sub == 7, 0.0, pltpu.roll(first, 7, 0))
                value = held[k]
                along = lon_ref[p, k] * value
                value = value + (above + below - (here + here)) + (sideways(along) - (along + along))
                below, here = here, above
                if number < PASSES - 1:
                    flip[1 - number % 2, k] = value
                else:
                    for j in range(STRIPS):
                        staged[p, j, pl.ds(k, 8, stride=STEP), :] = value[:, j * LANES : (j + 1) * LANES]
        for j in range(STRIPS):
            leaving(p, j).start()

    mean_ref[0, 0] = jnp.sum(cost_ref[...]) * (0.5 / (LAT * LON * CHANNELS))
    for p in range(PLANES):
        for j in range(STRIPS):
            leaving(p, j).wait()
    rad_copy.wait()


def shards(
    background, field_ids, filter_table, first_weight, first_bias, second_weight, second_bias,
    predictor_index, predictor_coef, channel_level, observed,
):
    vmem = pl.BlockSpec(memory_space=pltpu.VMEM)
    smem = pl.BlockSpec(memory_space=pltpu.SMEM)
    anywhere = pl.BlockSpec(memory_space=pl.ANY)
    dma = pltpu.SemaphoreType.DMA
    message = (CHUNKS, DEVICES, ROWS, LANES)
    coefs = jax.ShapeDtypeStruct((PLANES, STEP, 8, LON), F32)
    outcome = pl.pallas_call(
        forward_kernel,
        out_shape=(
            jax.ShapeDtypeStruct(message, BF16),
            coefs,
            coefs,
            jax.ShapeDtypeStruct((LON, CHANNELS), BF16),
            jax.ShapeDtypeStruct((DEVICES, 1, LANES), F32),
        ),
        in_specs=[anywhere, anywhere, smem, anywhere, vmem, anywhere, vmem, vmem, vmem, vmem, anywhere],
        out_specs=[vmem] * 5,
        scratch_shapes=[
            pltpu.VMEM((PLANES, STRIPS, LAT, LANES), F32),
            pltpu.VMEM((STRIPS, LAT, LANES), jnp.int32),
            pltpu.VMEM((2, STEP, 8, LON), F32),
            pltpu.VMEM((CHUNKS, DEVICES * ROWS, LANES), F32),
            pltpu.VMEM(message, BF16),
            pltpu.VMEM(message, BF16),
            pltpu.VMEM(message, BF16),
            pltpu.VMEM((FEATURES, UNITS), BF16),
            pltpu.VMEM((FEATURES, UNITS), BF16),
            pltpu.VMEM((UNITS, CHANNELS), BF16),
            pltpu.VMEM((LON, CHANNELS), F32),
            pltpu.VMEM((FEATURES, CHANNELS), F32),
            pltpu.VMEM((FEATURES, CHANNELS), BF16),
            pltpu.VMEM((FEATURES, CHANNELS), BF16),
            pltpu.VMEM((FEATURES, LANES), F32),
            pltpu.VMEM((8, LANES), F32),
            pltpu.VMEM((8, CHANNELS), F32),
            dma((PLANES, STRIPS)), dma((STRIPS,)), dma, dma, dma,
            dma((CHUNKS,)), dma((CHUNKS,)), dma((CHUNKS,)), dma((CHUNKS,)), dma((CHUNKS,)), dma, dma,
        ],
        compiler_params=pltpu.CompilerParams(
            collective_id=0, has_side_effects=True, vmem_limit_bytes=40 * 1024 * 1024
        ),
    )(
        background.reshape(PLANES, LAT, LON),
        field_ids,
        filter_table.reshape(64),
        first_weight,
        first_bias.reshape(1, UNITS),
        second_weight,
        second_bias.reshape(1, CHANNELS),
        predictor_index,
        predictor_coef,
        channel_level.reshape(CHANNELS, 1),
        observed.reshape(LON, CHANNELS),
    )
    gradient, radiances, mean_cost = pl.pallas_call(
        adjoint_kernel,
        out_shape=(
            jax.ShapeDtypeStruct((PLANES, LAT, LON), F32),
            jax.ShapeDtypeStruct((LON, CHANNELS), BF16),
            jax.ShapeDtypeStruct((1, 1), F32),
        ),
        in_specs=[vmem] * 5,
        out_specs=[anywhere, anywhere, smem],
        scratch_shapes=[
            pltpu.VMEM((CHUNKS, DEVICES * ROWS, LANES), F32),
            pltpu.VMEM((2, STEP, 8, LON), F32),
            pltpu.VMEM((PLANES, STRIPS, LAT, LANES), F32),
            dma,
            dma((PLANES, STRIPS)),
        ],
        compiler_params=pltpu.CompilerParams(vmem_limit_bytes=24 * 1024 * 1024),
    )(*outcome)
    return (
        radiances.reshape(1, LON, CHANNELS),
        mean_cost.reshape(()),
        gradient.reshape(2, 2, LAT, LON),
    )


def solution(mesh):
    placed = (
        P("lev", "var", None, None), P(), P(None, "lev", "var", None), P(), P(), P(), P(), P(), P(), P(),
        P(("lev", "var"), None, None),
    )
    return jax.shard_map(
        shards,
        mesh=mesh,
        in_specs=placed,
        out_specs=(P(("lev", "var"), None, None), P(), P("lev", "var", None, None)),
        check_vma=False,
    )
```

profile of v0, /device:TPU:1, one launch (start us, length us, event | category | flops | bytes accessed | tf_op | source)
XLA Modules:
  0.0 77.7 jit_solution(11702427747316757817)
XLA Ops:
  0.6 0.8 %copy.17 = f32[8,2,2,2]{3,2,1,0:T(2,128)S(1)} copy(f32[8,2,2,2]{0,3,2,1:T(2,128)} %param.13) | data formatting | bytes 512 | tf_op args[2]
  1.4 0.1 reshape.34.table_ref
  1.5 0.8 %copy.18.index_ref = s32[512,8]{1,0:T(8,128)S(1)} copy(s32[512,8]{0,1:T(8,128)} %param.18) | data formatting | bytes 32768 | tf_op args[7]
  2.4 0.8 %copy.19.coef_ref = f32[512,8]{1,0:T(8,128)S(1)} copy(f32[512,8]{0,1:T(8,128)} %param.19) | data formatting | bytes 32768 | tf_op args[8]
  3.2 0.8 %copy.20.level_ref = s32[512,1]{1,0:T(8,128)S(1)} copy(s32[512,1]{0,1:T(1,128)} %bitcast.12) | data formatting | bytes 4096 | tf_op jit(solution)/shard_map/reshape | solution.py:369
  4.1 0.0 copy-start
  4.1 1.6 %copy-done = f32[2,2,128,1024]{3,2,1,0:T(8,128)S(1)} copy-done((f32[2,2,128,1024]{3,2,1,0:T(8,128)S(1)}, f32[2,2,128,1024]{3,2,1,0:T(8,128)}, u32[]{:S(2)}) %copy-start) | copy-done | bytes 2097176
  5.7 0.0 copy-start.1
  5.7 1.6 %copy-done.1 = f32[1,1024,512]{2,1,0:T(8,128)S(1)} copy-done((f32[1,1024,512]{2,1,0:T(8,128)S(1)}, f32[1,1024,512]{2,1,0:T(8,128)}, u32[]{:S(2)}) %copy-start.1) | copy-done | bytes 2097176
  7.3 0.0 copy-start.2
  7.3 1.2 %copy-done.2 = bf16[512,1024]{1,0:T(8,128)(2,1)S(1)} copy-done((bf16[512,1024]{1,0:T(8,128)(2,1)S(1)}, bf16[512,1024]{1,0:T(8,128)(2,1)}, u32[]{:S(2)}) %copy-start.2) | copy-done | bytes 1048600
  8.5 0.0 copy-start.3
  8.5 1.2 %copy-done.3 = bf16[1024,512]{1,0:T(8,128)(2,1)S(1)} copy-done((bf16[1024,512]{1,0:T(8,128)(2,1)S(1)}, bf16[1024,512]{1,0:T(8,128)(2,1)}, u32[]{:S(2)}) %copy-start.3) | copy-done | bytes 1048600
  9.7 0.0 copy-start.4
  9.7 1.0 %copy-done.4 = s32[128,1024]{1,0:T(8,128)S(1)} copy-done((s32[128,1024]{1,0:T(8,128)S(1)}, s32[128,1024]{1,0:T(8,128)}, u32[]{:S(2)}) %copy-start.4) | copy-done | bytes 524312
  10.7 0.0 copy-start.5
  10.7 0.7 copy-done.5
  11.4 0.0 copy-start.6
  11.4 0.7 copy-done.6
  12.1 56.5 %shard_map.130 = (bf16[2,128,16,128]{3,2,1,0:T(8,128)(2,1)S(1)}, f32[4,16,8,1024]{3,2,1,0:T(8,128)S(1)}, f32[4,16,8,1024]{3,2,1,0:T(8,128)S(1)}, bf16[1024,512]{1,0:T(8,128)(2,1)S(1)}, f32[128,1,128]{2,1,0:T(1,128)S(1)}) custom-call(f32[4,128,1024]{2,1,0:T(8,128)S(1)} %bitcast.8, s32[128,1024]{1,0:T(8,128)S(1)} %copy-done.4, f32[64]{0:T(128)S(1)} %reshape.34.table_ref, ...), custom_call_target="tpu_custom_call" | custom-call | tf_op jit(solution)/shard_map/pallas_call | solution.py:324
  68.6 8.9 %shard_map.131 = (f32[4,128,1024]{2,1,0:T(8,128)}, bf16[1024,512]{1,0:T(8,128)(2,1)}, f32[1,1]{1,0:T(1,128)}) custom-call(bf16[2,128,16,128]{3,2,1,0:T(8,128)(2,1)S(1)} %get-tuple-element.11.back_ref, f32[4,16,8,1024]{3,2,1,0:T(8,128)S(1)} %get-tuple-element.12.lat_ref, f32[4,16,8,1024]{3,2,1,0:T(8,128)S(1)} %get-tuple-element.13.lon_ref, ...), custom_call_target="tpu_custom_call" | custom-call | tf_op jit(solution)/shard_map/pallas_call | solution.py:372
Async XLA Ops:
  4.1 1.6 %copy-start = (f32[2,2,128,1024]{3,2,1,0:T(8,128)S(1)}, f32[2,2,128,1024]{3,2,1,0:T(8,128)}, u32[]{:S(2)}) copy-start(f32[2,2,128,1024]{3,2,1,0:T(8,128)} %param.11) | copy-start | bytes 6291460
  5.7 1.6 %copy-start.1 = (f32[1,1024,512]{2,1,0:T(8,128)S(1)}, f32[1,1024,512]{2,1,0:T(8,128)}, u32[]{:S(2)}) copy-start(f32[1,1024,512]{2,1,0:T(8,128)} %param.21) | copy-start | bytes 6291460
  7.3 1.2 %copy-start.2 = (bf16[512,1024]{1,0:T(8,128)(2,1)S(1)}, bf16[512,1024]{1,0:T(8,128)(2,1)}, u32[]{:S(2)}) copy-start(bf16[512,1024]{1,0:T(8,128)(2,1)} %w1_ref.1) | copy-start | bytes 3145732
  8.5 1.2 %copy-start.3 = (bf16[1024,512]{1,0:T(8,128)(2,1)S(1)}, bf16[1024,512]{1,0:T(8,128)(2,1)}, u32[]{:S(2)}) copy-start(bf16[1024,512]{1,0:T(8,128)(2,1)} %w2_ref.1) | copy-start | bytes 3145732
  9.7 1.0 %copy-start.4 = (s32[128,1024]{1,0:T(8,128)S(1)}, s32[128,1024]{1,0:T(8,128)}, u32[]{:S(2)}) copy-start(s32[128,1024]{1,0:T(8,128)} %ids_ref.1) | copy-start | bytes 1572868
  10.7 0.7 copy-start.5
  11.4 0.7 copy-start.6
where the time goes:
time: 78.2 us; the launch traced here: 77.7 us
  Pallas kernels  65.4 us (84%)
  local copies, waits for them, and re-layouts  11.4 us (15%)
  between operations  0.84 us (1%)
    pallas_call x1, Pallas kernels, shards(): pl.pallas_call(forward_kernel, out_shape=(jax.ShapeDtypeStruct(message, B...  56.5 us
    unnamed x17, local copies, waits for them, and re-layouts  10.5 us
    pallas_call x1, Pallas kernels, shards(): pl.pallas_call(adjoint_kernel, out_shape=(jax.ShapeDtypeStruct((PLANES, L...  8.87 us

commit v1 on v0

--- a/solution.py
+++ b/solution.py
@@ -10,14 +10,17 @@
 PASSES = 4
 DEVICES = 128
 PLANES = 4
+FIELDS = 8
+TERMS = 8
 LAT, LON = 128, 1024
 STEP = 16
 LANES = 128
 STRIPS = 1024 // LANES
-NQ = 4
+NQ = 2
 CHUNKS = LON // (LANES * NQ)
 ROWS = PLANES * NQ
 COLS = LANES * NQ
+BLOCK = 256
 FEATURES, UNITS, CHANNELS = 512, 1024, 512
 MESH = pl.DeviceIdType.MESH
 F32, BF16 = jnp.float32, jnp.bfloat16
@@ -77,52 +80,20 @@
     return pltpu.roll(value, 1, 1) + pltpu.roll(value, LON - 1, 1)
 
 
-def forward_kernel(
-    grid_ref, ids_ref, table_ref, w1_ref, b1_ref, w2_ref, b2_ref, index_ref, coef_ref, level_ref, seen_ref,
-    back_ref, lat_ref, lon_ref, rad_ref, cost_ref,
-    planes, ids, flip, mixed, send, got, send_back, w1raw, w1, w2, obs, wide, sel_hi, sel_lo, turned,
-    active_ref, total,
-    grid_sem, ids_sem, w1_sem, w2_sem, obs_sem, own_sem, out1, in1, out2, in2, out3, in3,
-):
-    me, peers = targets()
-    barrier = pltpu.get_barrier_semaphore()
-    for lev, var in peers:
-        pl.semaphore_signal(barrier, 1, device_id=(lev, var), device_id_type=MESH)
-    strips = [pl.ds(j * LANES, LANES) for j in range(STRIPS)]
-    ids_copies = [pltpu.make_async_copy(ids_ref.at[:, s], ids.at[j], ids_sem.at[j]) for j, s in enumerate(strips)]
-    for copy in ids_copies:
-        copy.start()
-    grid_copies = [
-        pltpu.make_async_copy(grid_ref.at[p, :, s], planes.at[p, j], grid_sem.at[p, j])
-        for p in range(PLANES)
-        for j, s in enumerate(strips)
-    ]
-    for copy in grid_copies:
-        copy.start()
-    w1_copy = pltpu.make_async_copy(w1_ref, w1raw, w1_sem)
-    w2_copy = pltpu.make_async_copy(w2_ref, w2, w2_sem)
-    obs_copy = pltpu.make_async_copy(seen_ref, obs, obs_sem)
-    w1_copy.start()
-    w2_copy.start()
-    obs_copy.start()
-
-    for copy in ids_copies:
-        copy.wait()
-
+def coefficient_fields(ids, table_ref, lat_ref, lon_ref):
     @pl.loop(0, STEP)
     def _(k):
         field = gather_rows([ids.at[j] for j in range(STRIPS)], k)
         bits = [(field & (1 << n)) != 0 for n in range(3)]
         for p in range(PLANES):
             for axis, where in ((0, lat_ref), (1, lon_ref)):
-                level = [table_ref[n * 8 + p * 2 + axis] for n in range(8)]
+                level = [table_ref[p, axis, n] for n in range(FIELDS)]
                 for bit in bits:
                     level = [jnp.where(bit, level[2 * n + 1], level[2 * n]) for n in range(len(level) // 2)]
                 where[p, k] = level[0]
 
-    for copy in grid_copies:
-        copy.wait()
-
+
+def smooth(planes, flip, lat_ref, lon_ref, mixed):
     @pl.loop(0, PLANES)
     def _(p):
         for k in range(STEP):
@@ -148,11 +119,128 @@
                                 mixed.at[c], k * ROWS + p * NQ + q, STEP * ROWS, value[:, at : at + LANES]
                             )
 
-    @pl.loop(0, CHUNKS)
-    def _(c):
-        @pl.loop(0, DEVICES, unroll=4)
-        def _(d):
-            send[c, d] = mixed[c, pl.ds(pl.multiple_of(d * ROWS, ROWS), ROWS), :].astype(BF16)
+
+def narrow(mixed, c, send):
+    @pl.loop(0, DEVICES, unroll=4)
+    def _(d):
+        send[c, d] = mixed[c, pl.ds(pl.multiple_of(d * ROWS, ROWS), ROWS), :].astype(BF16)
+
+
+def widen(got, c, mixed):
+    @pl.loop(0, DEVICES, unroll=4)
+    def _(d):
+        mixed[c, pl.ds(pl.multiple_of(d * ROWS, ROWS), ROWS), :] = got[c, d].astype(F32)
+
+
+def selection(index_ref, coef_ref, level_ref, sel_hi, sel_lo):
+    @pl.loop(0, FEATURES // 64)
+    def _(group):
+        row = lax.broadcasted_iota(jnp.int32, (64, CHANNELS), 0)
+        feature = row * 8 + (group // 4) * 4 + (group % 2) * 2 + (group // 2) % 2
+        picks = jnp.where(feature // 4 == level_ref[...], 1.0, 0.0).astype(F32)
+        for n in range(TERMS):
+            picks = picks + jnp.where(feature == index_ref[n : n + 1, :], coef_ref[n : n + 1, :], 0.0)
+        high = picks.astype(BF16)
+        at = pl.ds(pl.multiple_of(group * 64, 64), 64)
+        sel_hi[at, :] = high
+        sel_lo[at, :] = (picks - high.astype(F32)).astype(BF16)
+
+
+def regroup(w1raw, turned, w1):
+    for part in range(UNITS // LANES):
+        turned[...] = w1raw[:, part * LANES : (part + 1) * LANES].astype(F32)
+        for s in range(8):
+            block = turned[pl.ds(s, 64, stride=8), :]
+            at = ((s // 4) * 2 + s % 2) * LANES + ((s // 2) % 2) * 64
+            w1[at : at + 64, part * LANES : (part + 1) * LANES] = block.astype(BF16)
+
+
+def network(c, mixed, turned, w1, b1_ref, w2, b2_ref, sel_hi, sel_lo, obs, rad_ref, total):
+    for part in range(COLS // BLOCK):
+        tiles = range(part * BLOCK // LANES, (part + 1) * BLOCK // LANES)
+        for n, q in enumerate(tiles):
+            for p in range(PLANES):
+                for var in range(2):
+                    block = mixed[c, pl.ds(var * ROWS + p * NQ + q, 64, stride=2 * ROWS), :]
+                    at = p * LANES + var * 64
+                    turned[at : at + 64, n * LANES : (n + 1) * LANES] = block
+        columns = turned[...].T.astype(BF16)
+        spot = pl.ds(pl.multiple_of(c * COLS + part * BLOCK, BLOCK), BLOCK)
+        active = jnp.tanh(jnp.dot(columns, w1[...], preferred_element_type=F32) + b1_ref[...])
+        evolved = jnp.dot(active.astype(BF16), w2[...], preferred_element_type=F32) + b2_ref[...]
+        evolved = evolved + jnp.dot(columns, sel_hi[...], preferred_element_type=F32)
+        evolved = evolved + jnp.dot(columns, sel_lo[...], preferred_element_type=F32)
+        rad_ref[spot, :] = evolved.astype(BF16)
+        depart = evolved - obs[spot, :]
+        total[...] += jnp.sum((depart * depart).reshape(BLOCK // 8, 8, CHANNELS), axis=0)
+        depart_hi = depart.astype(BF16)
+        depart_lo = (depart - depart_hi.astype(F32)).astype(BF16)
+        turn = (((1,), (1,)), ((), ()))
+        pull = lax.dot_general(depart_hi, w2[...], turn, preferred_element_type=F32)
+        pull = (pull * (1.0 - active * active)).astype(BF16)
+        slope = lax.dot_general(w1[...], pull, turn, preferred_element_type=F32)
+        slope = slope + lax.dot_general(sel_hi[...], depart_hi, turn, preferred_element_type=F32)
+        slope = slope + lax.dot_general(sel_lo[...], depart_hi, turn, preferred_element_type=F32)
+        slope = slope + lax.dot_general(sel_hi[...], depart_lo, turn, preferred_element_type=F32)
+        for n, q in enumerate(tiles):
+            for p in range(PLANES):
+                for var in range(2):
+                    at = p * LANES + var * 64
+                    block = slope[at : at + 64, n * LANES : (n + 1) * LANES]
+                    mixed[c, pl.ds(var * ROWS + p * NQ + q, 64, stride=2 * ROWS), :] = block
+
+
+def forward_kernel(
+    grid_ref, ids_ref, table_hbm, w1_ref, b1_hbm, w2_ref, b2_hbm, index_hbm, coef_hbm, level_hbm, seen_ref,
+    back_ref, lat_ref, lon_ref, rad_ref, cost_ref,
+    planes, ids, flip, mixed, send, got, send_back, w1raw, w1, w2, obs, sel_hi, sel_lo, strip, turned,
+    table_ref, b1_ref, b2_ref, index_ref, coef_ref, level_ref, total,
+    grid_sem, ids_sem, table_sem, small_sem, w1_sem, w2_sem, obs_sem, own_sem, out1, in1, out2, in2, out3, in3,
+):
+    me, peers = targets()
+    barrier = pltpu.get_barrier_semaphore()
+    for lev, var in peers:
+        pl.semaphore_signal(barrier, 1, device_id=(lev, var), device_id_type=MESH)
+    strips = [pl.ds(j * LANES, LANES) for j in range(STRIPS)]
+    ids_copies = [pltpu.make_async_copy(ids_ref.at[:, s], ids.at[j], ids_sem.at[j]) for j, s in enumerate(strips)]
+    for copy in ids_copies:
+        copy.start()
+    table_copy = pltpu.make_async_copy(table_hbm, table_ref, table_sem)
+    table_copy.start()
+    grid_copies = [
+        pltpu.make_async_copy(grid_ref.at[p, :, s], planes.at[p, j], grid_sem.at[p, j])
+        for p in range(PLANES)
+        for j, s in enumerate(strips)
+    ]
+    for copy in grid_copies:
+        copy.start()
+    w1_copy = pltpu.make_async_copy(w1_ref, w1raw, w1_sem)
+    w2_copy = pltpu.make_async_copy(w2_ref, w2, w2_sem)
+    obs_copy = pltpu.make_async_copy(seen_ref, obs, obs_sem)
+    small_copies = [
+        pltpu.make_async_copy(here, there, small_sem.at[n])
+        for n, (here, there) in enumerate(
+            (
+                (index_hbm, index_ref), (coef_hbm, coef_ref), (level_hbm, level_ref), (b1_hbm, b1_ref), (b2_hbm, b2_ref)
+            )
+        )
+    ]
+    for copy in small_copies:
+        copy.start()
+    w1_copy.start()
+    w2_copy.start()
+    obs_copy.start()
+
+    for copy in ids_copies:
+        copy.wait()
+    table_copy.wait()
+    coefficient_fields(ids, table_ref, lat_ref, lon_ref)
+    for copy in grid_copies:
+        copy.wait()
+
+    smooth(planes, flip, lat_ref, lon_ref, mixed)
+    for c in range(CHUNKS):
+        narrow(mixed, c, send)
 
     pl.semaphore_wait(barrier, DEVICES - 1)
 
@@ -165,23 +253,11 @@
             ).start()
         pltpu.make_async_copy(send.at[c, me], got.at[c, me], own_sem.at[c]).start()
 
-    row = lax.broadcasted_iota(jnp.int32, (CHANNELS, FEATURES), 1)
-    feature = (row % 64) * 8 + (row // 256) * 4 + ((row // 64) % 2) * 2 + (row // 128) % 2
-    picks = jnp.where(feature // 4 == level_ref[...], 1.0, 0.0).astype(F32)
-    for n in range(8):
-        picks = picks + jnp.where(feature == index_ref[:, n : n + 1], coef_ref[:, n : n + 1], 0.0)
-    wide[0:FEATURES, 0:CHANNELS] = picks.T
-    picks = wide[0:FEATURES, 0:CHANNELS]
-    high = picks.astype(BF16)
-    sel_hi[...] = high
-    sel_lo[...] = (picks - high.astype(F32)).astype(BF16)
+    for copy in small_copies:
+        copy.wait()
+    selection(index_ref, coef_ref, level_ref, sel_hi, sel_lo)
     w1_copy.wait()
-    for part in range(UNITS // LANES):
-        turned[0:FEATURES, :] = w1raw[:, part * LANES : (part + 1) * LANES].astype(F32)
-        for s in range(8):
-            block = turned[pl.ds(s, 64, stride=8), :]
-            at = ((s // 4) * 2 + s % 2) * LANES + ((s // 2) % 2) * 64
-            w1[at : at + 64, part * LANES : (part + 1) * LANES] = block.astype(BF16)
+    regroup(w1raw, strip, w1)
     w2_copy.wait()
     obs_copy.wait()
     total[...] = jnp.zeros_like(total)
@@ -192,43 +268,9 @@
         others = pl.ds(0, DEVICES - 1)
         pltpu.make_async_copy(got.at[c, others], got.at[c, others], in1.at[c]).wait()
 
-        @pl.loop(0, DEVICES, unroll=4)
-        def _(d):
-            mixed[c, pl.ds(pl.multiple_of(d * ROWS, ROWS), ROWS), :] = got[c, d].astype(F32)
-
-        for q in range(NQ):
-            for p in range(PLANES):
-                for var in range(2):
-                    block = mixed[c, pl.ds(var * ROWS + p * NQ + q, 64, stride=2 * ROWS), :]
-                    turned[p * LANES + var * 64 : p * LANES + var * 64 + 64, :] = block
-            columns = turned[...].T.astype(BF16)
-            first = pl.multiple_of(c * COLS + q * LANES, LANES)
-            spot = pl.ds(first, LANES)
-            active = jnp.tanh(jnp.dot(columns, w1[...], preferred_element_type=F32) + b1_ref[...])
-            evolved = jnp.dot(active.astype(BF16), w2[...], preferred_element_type=F32) + b2_ref[...]
-            evolved = evolved + jnp.dot(columns, sel_hi[...], preferred_element_type=F32)
-            evolved = evolved + jnp.dot(columns, sel_lo[...], preferred_element_type=F32)
-            rad_ref[spot, :] = evolved.astype(BF16)
-            depart = evolved - obs[spot, :]
-            total[...] += jnp.sum((depart * depart).reshape(LANES // 8, 8, CHANNELS), axis=0)
-            depart_hi = depart.astype(BF16)
-            depart_lo = (depart - depart_hi.astype(F32)).astype(BF16)
-            turn = (((1,), (1,)), ((), ()))
-            pull = lax.dot_general(depart_hi, w2[...], turn, preferred_element_type=F32)
-            pull = (pull * (1.0 - active * active)).astype(BF16)
-            slope = lax.dot_general(w1[...], pull, turn, preferred_element_type=F32)
-            slope = slope + lax.dot_general(sel_hi[...], depart_hi, turn, preferred_element_type=F32)
-            slope = slope + lax.dot_general(sel_lo[...], depart_hi, turn, preferred_element_type=F32)
-            slope = slope + lax.dot_general(sel_hi[...], depart_lo, turn, preferred_element_type=F32)
-            for p in range(PLANES):
-                for var in range(2):
-                    at = p * LANES + var * 64
-                    mixed[c, pl.ds(var * ROWS + p * NQ + q, 64, stride=2 * ROWS), :] = slope[at : at + 64]
-
-        @pl.loop(0, DEVICES, unroll=4)
-        def _(d):
-            send_back[c, d] = mixed[c, pl.ds(pl.multiple_of(d * ROWS, ROWS), ROWS), :].astype(BF16)
-
+        widen(got, c, mixed)
+        network(c, mixed, turned, w1, b1_ref, w2, b2_ref, sel_hi, sel_lo, obs, rad_ref, total)
+        narrow(mixed, c, send_back)
         for lev, var in peers:
             pltpu.make_async_remote_copy(
                 send_back.at[c, lev * 2 + var], back_ref.at[c, me], out2.at[c], in2.at[c],
@@ -266,10 +308,7 @@
         return pltpu.make_async_copy(staged.at[p, j], grad_ref.at[p, :, strip], grad_sem.at[p, j])
 
     for c in range(CHUNKS):
-
-        @pl.loop(0, DEVICES, unroll=4)
-        def _(d):
-            mixed[c, pl.ds(pl.multiple_of(d * ROWS, ROWS), ROWS), :] = back_ref[c, d].astype(F32)
+        widen(back_ref, c, mixed)
 
     @pl.loop(0, PLANES)
     def _(p):
@@ -317,7 +356,7 @@
 ):
     vmem = pl.BlockSpec(memory_space=pltpu.VMEM)
     smem = pl.BlockSpec(memory_space=pltpu.SMEM)
-    anywhere = pl.BlockSpec(memory_space=pl.ANY)
+    anywhere = pl.BlockSpec(memory_space=pltpu.HBM)
     dma = pltpu.SemaphoreType.DMA
     message = (CHUNKS, DEVICES, ROWS, LANES)
     coefs = jax.ShapeDtypeStruct((PLANES, STEP, 8, LON), F32)
@@ -330,7 +369,7 @@
             jax.ShapeDtypeStruct((LON, CHANNELS), BF16),
             jax.ShapeDtypeStruct((DEVICES, 1, LANES), F32),
         ),
-        in_specs=[anywhere, anywhere, smem, anywhere, vmem, anywhere, vmem, vmem, vmem, vmem, anywhere],
+        in_specs=[anywhere] * 11,
         out_specs=[vmem] * 5,
         scratch_shapes=[
             pltpu.VMEM((PLANES, STRIPS, LAT, LANES), F32),
@@ -344,30 +383,40 @@
             pltpu.VMEM((FEATURES, UNITS), BF16),
             pltpu.VMEM((UNITS, CHANNELS), BF16),
             pltpu.VMEM((LON, CHANNELS), F32),
-            pltpu.VMEM((FEATURES, CHANNELS), F32),
             pltpu.VMEM((FEATURES, CHANNELS), BF16),
             pltpu.VMEM((FEATURES, CHANNELS), BF16),
             pltpu.VMEM((FEATURES, LANES), F32),
-            pltpu.VMEM((8, LANES), F32),
+            pltpu.VMEM((FEATURES, BLOCK), F32),
+            pltpu.SMEM((PLANES, 2, FIELDS), F32),
+            pltpu.VMEM((1, UNITS), F32),
+            pltpu.VMEM((1, CHANNELS), F32),
+            pltpu.VMEM((TERMS, CHANNELS), jnp.int32),
+            pltpu.VMEM((TERMS, CHANNELS), F32),
+            pltpu.VMEM((1, CHANNELS), jnp.int32),
             pltpu.VMEM((8, CHANNELS), F32),
-            dma((PLANES, STRIPS)), dma((STRIPS,)), dma, dma, dma,
+            dma((PLANES, STRIPS)), dma((STRIPS,)), dma, dma((5,)), dma, dma, dma,
             dma((CHUNKS,)), dma((CHUNKS,)), dma((CHUNKS,)), dma((CHUNKS,)), dma((CHUNKS,)), dma, dma,
         ],
         compiler_params=pltpu.CompilerParams(
             collective_id=0, has_side_effects=True, vmem_limit_bytes=40 * 1024 * 1024
         ),
     )(
-        background.reshape(PLANES, LAT, LON),
-        field_ids,
-        filter_table.reshape(64),
-        first_weight,
-        first_bias.reshape(1, UNITS),
-        second_weight,
-        second_bias.reshape(1, CHANNELS),
-        predictor_index,
-        predictor_coef,
-        channel_level.reshape(CHANNELS, 1),
-        observed.reshape(LON, CHANNELS),
+        *(
+            pltpu.with_memory_space_constraint(operand, pltpu.HBM)
+            for operand in (
+                background.reshape(PLANES, LAT, LON),
+                field_ids,
+                filter_table.transpose(1, 2, 3, 0).reshape(PLANES, 2, FIELDS),
+                first_weight,
+                first_bias.reshape(1, UNITS),
+                second_weight,
+                second_bias.reshape(1, CHANNELS),
+                predictor_index.T,
+                predictor_coef.T,
+                channel_level.reshape(1, CHANNELS),
+                observed.reshape(LON, CHANNELS),
+            )
+        )
     )
     gradient, radiances, mean_cost = pl.pallas_call(
         adjoint_kernel,

time: 78.2 us -> 56.6 us (0.72)
  local copies, waits for them, and re-layouts: 11.4 us -> 0 us
  Pallas kernels: 65.4 us -> 55.8 us
    unnamed x17 -> x0, local copies, waits for them, and re-layouts: 10.5 us -> none
    pallas_call x1, Pallas kernels: 56.5 us -> 47.2 us  [shards(): pl.pallas_call(forward_kernel, out_shape=(jax.ShapeDtypeStruct(message, B...]
    reshape x2 -> x0, local copies, waits for them, and re-layouts: 0.94 us -> none  [the longest x1 0.82 us: shards(): channel_level.reshape(CHANNELS, 1)]
where the time goes in v1:
time: 56.6 us; the launch traced here: 56.5 us
  Pallas kernels  55.8 us (99%)
  between operations  0.64 us (1%)
    pallas_call x1, Pallas kernels, shards(): pl.pallas_call(forward_kernel, out_shape=(jax.ShapeDtypeStruct(message, B...  47.2 us
    pallas_call x1, Pallas kernels, shards(): pl.pallas_call(adjoint_kernel, out_shape=(jax.ShapeDtypeStruct((PLANES, L...  8.64 us

profile of v1, /device:TPU:1, one launch (start us, length us, event | category | flops | bytes accessed | tf_op | source)
XLA Modules:
  0.0 56.5 jit_solution(14312919104666269749)
XLA Ops:
  0.6 47.2 %shard_map.130 = (bf16[4,128,8,128]{3,2,1,0:T(8,128)(2,1)S(1)}, f32[4,16,8,1024]{3,2,1,0:T(8,128)S(1)}, f32[4,16,8,1024]{3,2,1,0:T(8,128)S(1)}, bf16[1024,512]{1,0:T(8,128)(2,1)S(1)}, f32[128,1,128]{2,1,0:T(1,128)S(1)}) custom-call(f32[4,128,1024]{2,1,0:T(8,128)} %bitcast.13, s32[128,1024]{1,0:T(8,128)} %ids_ref.1, f32[4,2,8]{2,1,0:T(2,128)} %bitcast.17, ...), custom_call_target="tpu_custom_call" | custom-call | tf_op jit(solution)/shard_map/pallas_call | solution.py:363
  47.8 8.6 %shard_map.131 = (f32[4,128,1024]{2,1,0:T(8,128)}, bf16[1024,512]{1,0:T(8,128)(2,1)}, f32[1,1]{1,0:T(1,128)}) custom-call(bf16[4,128,8,128]{3,2,1,0:T(8,128)(2,1)S(1)} %get-tuple-element.11.back_ref, f32[4,16,8,1024]{3,2,1,0:T(8,128)S(1)} %get-tuple-element.12.lat_ref, f32[4,16,8,1024]{3,2,1,0:T(8,128)S(1)} %get-tuple-element.13.lon_ref, ...), custom_call_target="tpu_custom_call" | custom-call | tf_op jit(solution)/shard_map/pallas_call | solution.py:421

commit v2 on v1

v2 whole, which is shorter than its diff:
```python
import functools

import jax
import jax.numpy as jnp
from jax import lax
from jax.experimental import pallas as pl
from jax.experimental.pallas import tpu as pltpu
from jax.sharding import PartitionSpec as P

PASSES = 4
DEVICES = 128
PLANES = 4
FIELDS = 8
TERMS = 8
LAT, LON = 128, 1024
STEP = 16
LANES = 128
STRIPS = 1024 // LANES
NQ = 2
CHUNKS = LON // (LANES * NQ)
ROWS = PLANES * NQ
COLS = LANES * NQ
BLOCK = 256
FEATURES, UNITS, CHANNELS = 512, 1024, 512
MESH = pl.DeviceIdType.MESH
F32, BF16 = jnp.float32, jnp.bfloat16


def offset_of(number):
    return (number // 32, (number // 8) % 4, (number // 2) % 4, number % 2)


def hops_of(number):
    return sum(min(part, 4 - part) for part in offset_of(number)[:3])


ORDER = sorted(range(1, DEVICES), key=lambda n: (-hops_of(n), (n * 73 + 19) * 2654435761 % 4294967291))


def targets():
    lev, var = lax.axis_index("lev"), lax.axis_index("var")
    z, high, y, core = lev // 16, (lev // 8) % 2, (lev // 2) % 4, lev % 2
    x = high * 2 + var
    zs = [((z + d) % 4) * 16 for d in range(4)]
    ys = [((y + d) % 4) * 2 for d in range(4)]
    xs = [(x + d) % 4 for d in range(4)]
    cores = [(core + d) % 2 for d in range(2)]
    zy = [[a + b for b in ys] for a in zs]
    xc = [[(a // 2) * 8 + b for b in cores] for a in xs]
    low = [a % 2 for a in xs]
    found = []
    for number in ORDER:
        dz, dy, dx, dc = offset_of(number)
        found.append((zy[dz][dy] + xc[dx][dc], low[dx]))
    near = [(z * 16 + y * 2 + b + (a // 2) * 8, a % 2) for n, (a, b) in enumerate((a, b) for a in xs for b in cores) if n]
    far = [(c + high * 8 + core, var) for n, c in enumerate(c for row in zy for c in row) if n]
    return lev * 2 + var, found, (x * 2 + core, near), (z * 4 + y, far)


def scatter_rows(where, start, step, values):
    where[pl.ds(start, 8, stride=step), :] = values


def gather_rows(strips, k):
    return jnp.concatenate([strip[pl.ds(k, 8, stride=STEP), :] for strip in strips], axis=1)


def neighbours(held, k):
    sub = lax.broadcasted_iota(jnp.int32, (8, LON), 0)
    if k < STEP - 1:
        above = held[k + 1]
    else:
        above = jnp.where(sub == 7, 0.0, pltpu.roll(held[0], 7, 0))
    if k > 0:
        below = held[k - 1]
    else:
        below = jnp.where(sub == 0, 0.0, pltpu.roll(held[STEP - 1], 1, 0))
    return above, below


def sideways(value):
    return pltpu.roll(value, 1, 1) + pltpu.roll(value, LON - 1, 1)


def coefficient_fields(p, ids, table_ref, lat_ref, lon_ref):
    lane = lax.broadcasted_iota(jnp.int32, (8, LANES), 0)
    for axis, where in ((0, lat_ref), (1, lon_ref)):
        table = jnp.zeros((8, LANES), F32)
        for n in range(FIELDS):
            table = jnp.where(lane == n, table_ref[p, axis, n], table)
        for k in range(STEP):
            for j in range(STRIPS):
                field = ids[j, pl.ds(k, 8, stride=STEP), :]
                where[p, k, :, j * LANES : (j + 1) * LANES] = jnp.take_along_axis(
                    table, field, axis=0, mode="promise_in_bounds"
                )


def smooth(p, planes, flip, lat_ref, lon_ref, mixed):
    for k in range(STEP):
        flip[0, k] = gather_rows([planes.at[p, j] for j in range(STRIPS)], k)
    for number in range(PASSES):
        held = flip.at[number % 2]
        for k in range(STEP):
            above, below = neighbours(held, k)
            value = held[k]
            twice = value + value
            value = (
                value
                + lat_ref[p, k] * (above + below - twice)
                + lon_ref[p, k] * (sideways(value) - twice)
            )
            if number < PASSES - 1:
                flip[1 - number % 2, k] = value
            else:
                for j in range(STRIPS):
                    scatter_rows(mixed.at[p], k * STRIPS + j, STEP * STRIPS, value[:, j * LANES : (j + 1) * LANES])


def narrow(mixed, c, send):
    @pl.loop(0, DEVICES, unroll=4)
    def _(d):
        send[c, d] = mixed[c, pl.ds(pl.multiple_of(d * ROWS, ROWS), ROWS), :].astype(BF16)


def widen(got, c, mixed):
    @pl.loop(0, DEVICES, unroll=4)
    def _(d):
        mixed[c, pl.ds(pl.multiple_of(d * ROWS, ROWS), ROWS), :] = got[c, d].astype(F32)


def selection(index_ref, coef_ref, level_ref, sel):
    @pl.loop(0, FEATURES // 64)
    def _(group):
        row = lax.broadcasted_iota(jnp.int32, (64, CHANNELS), 0)
        feature = row * 8 + (group // 4) * 4 + (group % 2) * 2 + (group // 2) % 2
        picks = jnp.where(feature // 4 == level_ref[...], 1.0, 0.0).astype(F32)
        for n in range(TERMS):
            picks = picks + jnp.where(feature == index_ref[n : n + 1, :], coef_ref[n : n + 1, :], 0.0)
        sel[pl.ds(pl.multiple_of(group * 64, 64), 64), :] = picks.astype(BF16)


def regroup(w1raw, turned, w1):
    for part in range(UNITS // LANES):
        turned[...] = w1raw[:, part * LANES : (part + 1) * LANES].astype(F32)
        for s in range(8):
            block = turned[pl.ds(s, 64, stride=8), :]
            at = ((s // 4) * 2 + s % 2) * LANES + ((s // 2) % 2) * 64
            w1[at : at + 64, part * LANES : (part + 1) * LANES] = block.astype(BF16)


def network(c, arrived, mixed, turned, w1, b1_ref, w2, b2_ref, sel, obs, rad_ref, total):
    for part in range(COLS // BLOCK):
        tiles = range(part * BLOCK // LANES, (part + 1) * BLOCK // LANES)
        for n, q in enumerate(tiles):
            for p in range(PLANES):
                for var in range(2):
                    block = arrived[p, pl.ds(var * STRIPS + c * NQ + q, 64, stride=2 * STRIPS), :]
                    at = p * LANES + var * 64
                    turned[at : at + 64, n * LANES : (n + 1) * LANES] = block
        columns = turned[...].T.astype(BF16)
        spot = pl.ds(pl.multiple_of(c * COLS + part * BLOCK, BLOCK), BLOCK)
        active = jnp.tanh(jnp.dot(columns, w1[...], preferred_element_type=F32) + b1_ref[...])
        evolved = jnp.dot(active.astype(BF16), w2[...], preferred_element_type=F32) + b2_ref[...]
        evolved = evolved + jnp.dot(columns, sel[...], preferred_element_type=F32)
        rad_ref[spot, :] = evolved.astype(BF16)
        depart = evolved - obs[spot, :]
        total[...] += jnp.sum((depart * depart).reshape(BLOCK // 8, 8, CHANNELS), axis=0)
        depart_low = depart.astype(BF16)
        turn = (((1,), (1,)), ((), ()))
        pull = lax.dot_general(depart_low, w2[...], turn, preferred_element_type=F32)
        pull = (pull * (1.0 - active * active)).astype(BF16)
        slope = lax.dot_general(w1[...], pull, turn, preferred_element_type=F32)
        slope = slope + lax.dot_general(sel[...], depart_low, turn, preferred_element_type=F32)
        for n, q in enumerate(tiles):
            for p in range(PLANES):
                for var in range(2):
                    at = p * LANES + var * 64
                    block = slope[at : at + 64, n * LANES : (n + 1) * LANES]
                    mixed[c, pl.ds(var * ROWS + p * NQ + q, 64, stride=2 * ROWS), :] = block


def forward_kernel(
    grid_ref, ids_ref, table_hbm, w1_ref, b1_hbm, w2_ref, b2_hbm, index_hbm, coef_hbm, level_hbm, seen_ref,
    back_ref, lat_ref, lon_ref, rad_ref, cost_ref,
    planes, ids, flip, arrived, mixed, send, got, send_back, back, near_ref, w1raw, w1, w2, obs, sel, strip, turned,
    table_ref, b1_ref, b2_ref, index_ref, coef_ref, level_ref, total,
    grid_sem, ids_sem, table_sem, small_sem, w1_sem, w2_sem, obs_sem, own_sem, out1, in1, out2, in2, out3, in3, out4, in4,
):
    me, peers, (near, near_peers), (far, far_peers) = targets()
    strips = [pl.ds(j * LANES, LANES) for j in range(STRIPS)]
    ids_copies = [pltpu.make_async_copy(ids_ref.at[:, s], ids.at[j], ids_sem.at[j]) for j, s in enumerate(strips)]
    for copy in ids_copies:
        copy.start()
    table_copy = pltpu.make_async_copy(table_hbm, table_ref, table_sem)
    table_copy.start()
    grid_copies = [
        pltpu.make_async_copy(grid_ref.at[p, :, s], planes.at[p, j], grid_sem.at[p, j])
        for p in range(PLANES)
        for j, s in enumerate(strips)
    ]
    for copy in grid_copies:
        copy.start()
    w1_copy = pltpu.make_async_copy(w1_ref, w1raw, w1_sem)
    w2_copy = pltpu.make_async_copy(w2_ref, w2, w2_sem)
    obs_copy = pltpu.make_async_copy(seen_ref, obs, obs_sem)
    small_copies = [
        pltpu.make_async_copy(here, there, small_sem.at[n])
        for n, (here, there) in enumerate(
            (
                (index_hbm, index_ref), (coef_hbm, coef_ref), (level_hbm, level_ref), (b1_hbm, b1_ref), (b2_hbm, b2_ref)
            )
        )
    ]
    for copy in small_copies:
        copy.start()
    w1_copy.start()
    w2_copy.start()
    obs_copy.start()

    barrier = pltpu.get_barrier_semaphore()
    for lev, var in peers:
        pl.semaphore_signal(barrier, 1, device_id=(lev, var), device_id_type=MESH)

    for copy in ids_copies:
        copy.wait()
    table_copy.wait()

    def outward(p):
        def one(lev, var):
            pltpu.make_async_remote_copy(
                send.at[p, lev * 2 + var], got.at[p, me], out1.at[p], in1.at[p],
                device_id=(lev, var), device_id_type=MESH,
            ).start()

        yield from (functools.partial(one, lev, var) for lev, var in peers)
        yield pltpu.make_async_copy(send.at[p, me], got.at[p, me], own_sem.at[p]).start

    def homeward(c):
        def one(lev, var):
            pltpu.make_async_remote_copy(
                send_back.at[c, lev * 2 + var], back.at[c, me], out2.at[c], in2.at[c],
                device_id=(lev, var), device_id_type=MESH,
            ).start()

        yield from (functools.partial(one, lev, var) for lev, var in peers)
        yield pltpu.make_async_copy(send_back.at[c, me], back.at[c, me], own_sem.at[c]).start

    @pl.loop(0, PLANES)
    def _(p):
        coefficient_fields(p, ids, table_ref, lat_ref, lon_ref)
        for j, s in enumerate(strips):
            pltpu.make_async_copy(grid_ref.at[p, :, s], planes.at[p, j], grid_sem.at[p, j]).wait()
        smooth(p, planes, flip, lat_ref, lon_ref, arrived)
        narrow(arrived, p, send)

        @pl.when(p == 0)
        def _():
            pl.semaphore_wait(barrier, DEVICES - 1)

        for start in outward(p):
            start()

    for copy in small_copies:
        copy.wait()
    selection(index_ref, coef_ref, level_ref, sel)
    w1_copy.wait()
    regroup(w1raw, strip, w1)
    w2_copy.wait()
    obs_copy.wait()
    total[...] = jnp.zeros_like(total)
    others = pl.ds(0, DEVICES - 1)

    @pl.loop(0, PLANES)
    def _(p):
        pltpu.make_async_copy(send.at[p, me], got.at[p, me], own_sem.at[p]).wait()
        pltpu.make_async_copy(got.at[p, others], got.at[p, others], in1.at[p]).wait()
        widen(got, p, arrived)

    def chunk(c):
        network(c, arrived, mixed, turned, w1, b1_ref, w2, b2_ref, sel, obs, rad_ref, total)
        narrow(mixed, c, send_back)

    @pl.loop(0, CHUNKS)
    def _(c):
        chunk(c)

        @pl.when(c == CHUNKS - 1)
        def _():
            summed = jnp.sum(total[...], axis=0, keepdims=True)
            near_ref[near] = sum(summed[:, n * LANES : (n + 1) * LANES] for n in range(CHANNELS // LANES))
            for lev, var in near_peers:
                pltpu.make_async_remote_copy(
                    near_ref.at[near], near_ref.at[near], out3, in3, device_id=(lev, var), device_id_type=MESH
                ).start()

        for start in homeward(c):
            start()

    pltpu.make_async_copy(near_ref.at[pl.ds(0, 7)], near_ref.at[pl.ds(0, 7)], out3).wait()
    pltpu.make_async_copy(near_ref.at[pl.ds(0, 7)], near_ref.at[pl.ds(0, 7)], in3).wait()
    cost_ref[far] = jnp.sum(near_ref[...], axis=0)
    for lev, var in far_peers:
        pltpu.make_async_remote_copy(
            cost_ref.at[far], cost_ref.at[far], out4, in4, device_id=(lev, var), device_id_type=MESH
        ).start()
    for c in range(CHUNKS):
        pltpu.make_async_copy(send_back.at[c, me], back.at[c, me], own_sem.at[c]).wait()
        pltpu.make_async_copy(back.at[c, others], back.at[c, others], in2.at[c]).wait()
        widen(back, c, back_ref)
    for c in range(CHUNKS):
        pltpu.make_async_copy(send_back.at[c, others], send_back.at[c, others], out2.at[c]).wait()
    for p in range(PLANES):
        pltpu.make_async_copy(send.at[p, others], send.at[p, others], out1.at[p]).wait()
    pltpu.make_async_copy(cost_ref.at[pl.ds(0, 15)], cost_ref.at[pl.ds(0, 15)], out4).wait()
    pltpu.make_async_copy(cost_ref.at[pl.ds(0, 15)], cost_ref.at[pl.ds(0, 15)], in4).wait()


def unsmooth(p, mixed, flip, lat_ref, lon_ref, staged):
    for k in range(STEP):
        pieces = [
            mixed[c, pl.ds(k * ROWS + p * NQ + q, 8, stride=STEP * ROWS), :]
            for c in range(CHUNKS)
            for q in range(NQ)
        ]
        flip[0, k] = jnp.concatenate(pieces, axis=1)
    for number in range(PASSES):
        held = flip.at[number % 2]
        sub = lax.broadcasted_iota(jnp.int32, (8, LON), 0)
        first = lat_ref[p, 0] * held[0]
        last = lat_ref[p, STEP - 1] * held[STEP - 1]
        below = jnp.where(sub == 0, 0.0, pltpu.roll(last, 1, 0))
        here = first
        for k in range(STEP):
            if k < STEP - 1:
                above = lat_ref[p, k + 1] * held[k + 1]
            else:
                above = jnp.where(sub == 7, 0.0, pltpu.roll(first, 7, 0))
            value = held[k]
            along = lon_ref[p, k] * value
            value = value + (above + below - (here + here)) + (sideways(along) - (along + along))
            below, here = here, above
            if number < PASSES - 1:
                flip[1 - number % 2, k] = value
            else:
                for j in range(STRIPS):
                    staged[p, j, pl.ds(k, 8, stride=STEP), :] = value[:, j * LANES : (j + 1) * LANES]


def unsmooth(p, mixed, flip, lat_ref, lon_ref, staged):
    for k in range(STEP):
        pieces = [
            mixed[c, pl.ds(k * ROWS + p * NQ + q, 8, stride=STEP * ROWS), :]
            for c in range(CHUNKS)
            for q in range(NQ)
        ]
        flip[0, k] = jnp.concatenate(pieces, axis=1)
    for number in range(PASSES):
        held = flip.at[number % 2]
        sub = lax.broadcasted_iota(jnp.int32, (8, LON), 0)
        first = lat_ref[p, 0] * held[0]
        last = lat_ref[p, STEP - 1] * held[STEP - 1]
        below = jnp.where(sub == 0, 0.0, pltpu.roll(last, 1, 0))
        here = first
        for k in range(STEP):
            if k < STEP - 1:
                above = lat_ref[p, k + 1] * held[k + 1]
            else:
                above = jnp.where(sub == 7, 0.0, pltpu.roll(first, 7, 0))
            value = held[k]
            along = lon_ref[p, k] * value
            value = value + (above + below - (here + here)) + (sideways(along) - (along + along))
            below, here = here, above
            if number < PASSES - 1:
                flip[1 - number % 2, k] = value
            else:
                for j in range(STRIPS):
                    staged[p, j, pl.ds(k, 8, stride=STEP), :] = value[:, j * LANES : (j + 1) * LANES]


def adjoint_kernel(
    back_ref, lat_ref, lon_ref, rad_ref, cost_ref,
    grad_ref, rad_out, mean_ref,
    flip, staged, rad_sem, grad_sem,
):
    rad_copy = pltpu.make_async_copy(rad_ref, rad_out, rad_sem)
    rad_copy.start()

    def leaving(p, j):
        strip = pl.ds(j * LANES, LANES)
        return pltpu.make_async_copy(staged.at[p, j], grad_ref.at[p, :, strip], grad_sem.at[p, j])

    @pl.loop(0, PLANES)
    def _(p):
        unsmooth(p, back_ref, flip, lat_ref, lon_ref, staged)
        for j in range(STRIPS):
            leaving(p, j).start()

    mean_ref[0, 0] = jnp.sum(cost_ref[...]) * (0.5 / (LAT * LON * CHANNELS))
    for p in range(PLANES):
        for j in range(STRIPS):
            leaving(p, j).wait()
    rad_copy.wait()


def shards(
    background, field_ids, filter_table, first_weight, first_bias, second_weight, second_bias,
    predictor_index, predictor_coef, channel_level, observed,
):
    vmem = pl.BlockSpec(memory_space=pltpu.VMEM)
    smem = pl.BlockSpec(memory_space=pltpu.SMEM)
    anywhere = pl.BlockSpec(memory_space=pltpu.HBM)
    dma = pltpu.SemaphoreType.DMA
    message = (CHUNKS, DEVICES, ROWS, LANES)
    coefs = jax.ShapeDtypeStruct((PLANES, STEP, 8, LON), F32)
    outcome = pl.pallas_call(
        forward_kernel,
        out_shape=(
            jax.ShapeDtypeStruct((CHUNKS, DEVICES * ROWS, LANES), F32),
            coefs,
            coefs,
            jax.ShapeDtypeStruct((LON, CHANNELS), BF16),
            jax.ShapeDtypeStruct((DEVICES // 8, 1, LANES), F32),
        ),
        in_specs=[anywhere] * 11,
        out_specs=[vmem] * 5,
        scratch_shapes=[
            pltpu.VMEM((PLANES, STRIPS, LAT, LANES), F32),
            pltpu.VMEM((STRIPS, LAT, LANES), jnp.int32),
            pltpu.VMEM((2, STEP, 8, LON), F32),
            pltpu.VMEM((PLANES, DEVICES * STRIPS, LANES), F32),
            pltpu.VMEM((CHUNKS, DEVICES * ROWS, LANES), F32),
            pltpu.VMEM((PLANES, DEVICES, STRIPS, LANES), BF16),
            pltpu.VMEM((PLANES, DEVICES, STRIPS, LANES), BF16),
            pltpu.VMEM(message, BF16),
            pltpu.VMEM(message, BF16),
            pltpu.VMEM((8, 1, LANES), F32),
            pltpu.VMEM((FEATURES, UNITS), BF16),
            pltpu.VMEM((FEATURES, UNITS), BF16),
            pltpu.VMEM((UNITS, CHANNELS), BF16),
            pltpu.VMEM((LON, CHANNELS), F32),
            pltpu.VMEM((FEATURES, CHANNELS), BF16),
            pltpu.VMEM((FEATURES, LANES), F32),
            pltpu.VMEM((FEATURES, BLOCK), F32),
            pltpu.SMEM((PLANES, 2, FIELDS), F32),
            pltpu.VMEM((1, UNITS), F32),
            pltpu.VMEM((1, CHANNELS), F32),
            pltpu.VMEM((TERMS, CHANNELS), jnp.int32),
            pltpu.VMEM((TERMS, CHANNELS), F32),
            pltpu.VMEM((1, CHANNELS), jnp.int32),
            pltpu.VMEM((8, CHANNELS), F32),
            dma((PLANES, STRIPS)), dma((STRIPS,)), dma, dma((5,)), dma, dma, dma,
            dma((PLANES,)), dma((PLANES,)), dma((PLANES,)), dma((CHUNKS,)), dma((CHUNKS,)), dma, dma, dma, dma,
        ],
        compiler_params=pltpu.CompilerParams(
            collective_id=0, has_side_effects=True, vmem_limit_bytes=40 * 1024 * 1024
        ),
    )(
        *(
            pltpu.with_memory_space_constraint(operand, pltpu.HBM)
            for operand in (
                background.reshape(PLANES, LAT, LON),
                field_ids,
                filter_table.transpose(1, 2, 3, 0).reshape(PLANES, 2, FIELDS),
                first_weight,
                first_bias.reshape(1, UNITS),
                second_weight,
                second_bias.reshape(1, CHANNELS),
                predictor_index.T,
                predictor_coef.T,
                channel_level.reshape(1, CHANNELS),
                observed.reshape(LON, CHANNELS),
            )
        )
    )
    gradient, radiances, mean_cost = pl.pallas_call(
        adjoint_kernel,
        out_shape=(
            jax.ShapeDtypeStruct((PLANES, LAT, LON), F32),
            jax.ShapeDtypeStruct((LON, CHANNELS), BF16),
            jax.ShapeDtypeStruct((1, 1), F32),
        ),
        in_specs=[vmem] * 5,
        out_specs=[anywhere, anywhere, smem],
        scratch_shapes=[
            pltpu.VMEM((2, STEP, 8, LON), F32),
            pltpu.VMEM((PLANES, STRIPS, LAT, LANES), F32),
            dma,
            dma((PLANES, STRIPS)),
        ],
        compiler_params=pltpu.CompilerParams(vmem_limit_bytes=24 * 1024 * 1024),
    )(*outcome)
    return (
        radiances.reshape(1, LON, CHANNELS),
        mean_cost.reshape(()),
        gradient.reshape(2, 2, LAT, LON),
    )


def solution(mesh):
    placed = (
        P("lev", "var", None, None), P(), P(None, "lev", "var", None), P(), P(), P(), P(), P(), P(), P(),
        P(("lev", "var"), None, None),
    )
    return jax.shard_map(
        shards,
        mesh=mesh,
        in_specs=placed,
        out_specs=(P(("lev", "var"), None, None), P(), P("lev", "var", None, None)),
        check_vma=False,
    )
```

time: 56.6 us -> 53.6 us (0.947)
  Pallas kernels: 55.8 us -> 52.9 us
    pallas_call x1, Pallas kernels: 47.2 us -> 45.1 us  [shards(): pl.pallas_call(forward_kernel, out_shape=(jax.ShapeDtypeStruct((CHUNKS, D...]
    pallas_call x1, Pallas kernels: 8.64 us -> 7.8 us  [shards(): pl.pallas_call(adjoint_kernel, out_shape=(jax.ShapeDtypeStruct((PLANES, L...]
where the time goes in v2:
time: 53.6 us; the launch traced here: 53.5 us
  Pallas kernels  52.9 us (99%)
  between operations  0.64 us (1%)
    pallas_call x1, Pallas kernels, shards(): pl.pallas_call(forward_kernel, out_shape=(jax.ShapeDtypeStruct((CHUNKS, D...  45.1 us
    pallas_call x1, Pallas kernels, shards(): pl.pallas_call(adjoint_kernel, out_shape=(jax.ShapeDtypeStruct((PLANES, L...  7.8 us

profile of v2, /device:TPU:1, one launch (start us, length us, event | category | flops | bytes accessed | tf_op | source)
XLA Modules:
  0.0 53.5 jit_solution(16607045879897623540)
XLA Ops:
  0.6 45.1 %shard_map.130 = (f32[4,1024,128]{2,1,0:T(8,128)S(1)}, f32[4,16,8,1024]{3,2,1,0:T(8,128)S(1)}, f32[4,16,8,1024]{3,2,1,0:T(8,128)S(1)}, bf16[1024,512]{1,0:T(8,128)(2,1)S(1)}, f32[16,1,128]{2,1,0:T(1,128)S(1)}) custom-call(f32[4,128,1024]{2,1,0:T(8,128)} %bitcast.13, s32[128,1024]{1,0:T(8,128)} %ids_ref.1, f32[4,2,8]{2,1,0:T(2,128)} %bitcast.17, ...), custom_call_target="tpu_custom_call" | custom-call | tf_op jit(solution)/shard_map/pallas_call | solution.py:416
  45.7 7.8 %shard_map.131 = (f32[4,128,1024]{2,1,0:T(8,128)}, bf16[1024,512]{1,0:T(8,128)(2,1)}, f32[1,1]{1,0:T(1,128)}) custom-call(f32[4,1024,128]{2,1,0:T(8,128)S(1)} %get-tuple-element.11.back_ref, f32[4,16,8,1024]{3,2,1,0:T(8,128)S(1)} %get-tuple-element.12.lat_ref, f32[4,16,8,1024]{3,2,1,0:T(8,128)S(1)} %get-tuple-element.13.lon_ref, ...), custom_call_target="tpu_custom_call" | custom-call | tf_op jit(solution)/shard_map/pallas_call | solution.py:476

commit v3 on v2

--- a/solution.py
+++ b/solution.py
@@ -118,13 +118,13 @@
 
 
 def narrow(mixed, c, send):
-    @pl.loop(0, DEVICES, unroll=4)
+    @pl.loop(0, DEVICES, unroll=16)
     def _(d):
         send[c, d] = mixed[c, pl.ds(pl.multiple_of(d * ROWS, ROWS), ROWS), :].astype(BF16)
 
 
 def widen(got, c, mixed):
-    @pl.loop(0, DEVICES, unroll=4)
+    @pl.loop(0, DEVICES, unroll=16)
     def _(d):
         mixed[c, pl.ds(pl.multiple_of(d * ROWS, ROWS), ROWS), :] = got[c, d].astype(F32)
 

time: 53.6 us -> 52.4 us (0.978)
  Pallas kernels: 52.9 us -> 51.6 us
    pallas_call x1, Pallas kernels: 45.1 us -> 43.8 us  [shards(): pl.pallas_call(forward_kernel, out_shape=(jax.ShapeDtypeStruct((CHUNKS, D...]
where the time goes in v3:
time: 52.4 us; the launch traced here: 52.2 us
  Pallas kernels  51.6 us (98%)
  between operations  0.64 us (1%)
    pallas_call x1, Pallas kernels, shards(): pl.pallas_call(forward_kernel, out_shape=(jax.ShapeDtypeStruct((CHUNKS, D...  43.8 us
    pallas_call x1, Pallas kernels, shards(): pl.pallas_call(adjoint_kernel, out_shape=(jax.ShapeDtypeStruct((PLANES, L...  7.8 us

profile of v3, /device:TPU:1, one launch (start us, length us, event | category | flops | bytes accessed | tf_op | source)
XLA Modules:
  0.0 52.2 jit_solution(14904491388059576543)
XLA Ops:
  0.6 43.8 %shard_map.130 = (f32[4,1024,128]{2,1,0:T(8,128)S(1)}, f32[4,16,8,1024]{3,2,1,0:T(8,128)S(1)}, f32[4,16,8,1024]{3,2,1,0:T(8,128)S(1)}, bf16[1024,512]{1,0:T(8,128)(2,1)S(1)}, f32[16,1,128]{2,1,0:T(1,128)S(1)}) custom-call(f32[4,128,1024]{2,1,0:T(8,128)} %bitcast.13, s32[128,1024]{1,0:T(8,128)} %ids_ref.1, f32[4,2,8]{2,1,0:T(2,128)} %bitcast.17, ...), custom_call_target="tpu_custom_call" | custom-call | tf_op jit(solution)/shard_map/pallas_call | solution.py:416
  44.4 7.8 %shard_map.131 = (f32[4,128,1024]{2,1,0:T(8,128)}, bf16[1024,512]{1,0:T(8,128)(2,1)}, f32[1,1]{1,0:T(1,128)}) custom-call(f32[4,1024,128]{2,1,0:T(8,128)S(1)} %get-tuple-element.11.back_ref, f32[4,16,8,1024]{3,2,1,0:T(8,128)S(1)} %get-tuple-element.12.lat_ref, f32[4,16,8,1024]{3,2,1,0:T(8,128)S(1)} %get-tuple-element.13.lon_ref, ...), custom_call_target="tpu_custom_call" | custom-call | tf_op jit(solution)/shard_map/pallas_call | solution.py:476

commit v4 on v3

--- a/solution.py
+++ b/solution.py
@@ -82,34 +82,33 @@
     return pltpu.roll(value, 1, 1) + pltpu.roll(value, LON - 1, 1)
 
 
-def coefficient_fields(p, ids, table_ref, lat_ref, lon_ref):
-    lane = lax.broadcasted_iota(jnp.int32, (8, LANES), 0)
-    for axis, where in ((0, lat_ref), (1, lon_ref)):
-        table = jnp.zeros((8, LANES), F32)
-        for n in range(FIELDS):
-            table = jnp.where(lane == n, table_ref[p, axis, n], table)
-        for k in range(STEP):
-            for j in range(STRIPS):
-                field = ids[j, pl.ds(k, 8, stride=STEP), :]
-                where[p, k, :, j * LANES : (j + 1) * LANES] = jnp.take_along_axis(
-                    table, field, axis=0, mode="promise_in_bounds"
-                )
-
-
-def smooth(p, planes, flip, lat_ref, lon_ref, mixed):
+def coefficients(field, levels):
+    bits = [(field & (1 << n)) != 0 for n in range(3)]
+    chosen = []
+    for level in levels:
+        for bit in bits:
+            level = [jnp.where(bit, level[2 * n + 1], level[2 * n]) for n in range(len(level) // 2)]
+        chosen.append(level[0])
+    return chosen
+
+
+def smooth(p, ids, table_ref, planes, flip, lat_ref, lon_ref, mixed):
+    levels = [[table_ref[p, axis, n] for n in range(FIELDS)] for axis in range(2)]
     for k in range(STEP):
         flip[0, k] = gather_rows([planes.at[p, j] for j in range(STRIPS)], k)
     for number in range(PASSES):
         held = flip.at[number % 2]
         for k in range(STEP):
+            if number == 0:
+                field = gather_rows([ids.at[j] for j in range(STRIPS)], k)
+                lat_coef, lon_coef = coefficients(field, levels)
+                lat_ref[p, k], lon_ref[p, k] = lat_coef, lon_coef
+            else:
+                lat_coef, lon_coef = lat_ref[p, k], lon_ref[p, k]
             above, below = neighbours(held, k)
             value = held[k]
             twice = value + value
-            value = (
-                value
-                + lat_ref[p, k] * (above + below - twice)
-                + lon_ref[p, k] * (sideways(value) - twice)
-            )
+            value = value + lat_coef * (above + below - twice) + lon_coef * (sideways(value) - twice)
             if number < PASSES - 1:
                 flip[1 - number % 2, k] = value
             else:
@@ -248,10 +247,9 @@
 
     @pl.loop(0, PLANES)
     def _(p):
-        coefficient_fields(p, ids, table_ref, lat_ref, lon_ref)
         for j, s in enumerate(strips):
             pltpu.make_async_copy(grid_ref.at[p, :, s], planes.at[p, j], grid_sem.at[p, j]).wait()
-        smooth(p, planes, flip, lat_ref, lon_ref, arrived)
+        smooth(p, ids, table_ref, planes, flip, lat_ref, lon_ref, arrived)
         narrow(arrived, p, send)
 
         @pl.when(p == 0)

time: 52.4 us -> 52.3 us (level)
  no operation moved by 1% of the time
where the time goes in v4:
time: 52.3 us; the launch traced here: 52.2 us
  Pallas kernels  51.6 us (99%)
  between operations  0.64 us (1%)
    pallas_call x1, Pallas kernels, shards(): pl.pallas_call(forward_kernel, out_shape=(jax.ShapeDtypeStruct((CHUNKS, D...  43.8 us
    pallas_call x1, Pallas kernels, shards(): pl.pallas_call(adjoint_kernel, out_shape=(jax.ShapeDtypeStruct((PLANES, L...  7.8 us

profile of v4, /device:TPU:1, one launch (start us, length us, event | category | flops | bytes accessed | tf_op | source)
XLA Modules:
  0.0 52.2 jit_solution(13462304915742208171)
XLA Ops:
  0.6 43.8 %shard_map.130 = (f32[4,1024,128]{2,1,0:T(8,128)S(1)}, f32[4,16,8,1024]{3,2,1,0:T(8,128)S(1)}, f32[4,16,8,1024]{3,2,1,0:T(8,128)S(1)}, bf16[1024,512]{1,0:T(8,128)(2,1)S(1)}, f32[16,1,128]{2,1,0:T(1,128)S(1)}) custom-call(f32[4,128,1024]{2,1,0:T(8,128)} %bitcast.13, s32[128,1024]{1,0:T(8,128)} %ids_ref.1, f32[4,2,8]{2,1,0:T(2,128)} %bitcast.17, ...), custom_call_target="tpu_custom_call" | custom-call | tf_op jit(solution)/shard_map/pallas_call | solution.py:414
  44.4 7.8 %shard_map.131 = (f32[4,128,1024]{2,1,0:T(8,128)}, bf16[1024,512]{1,0:T(8,128)(2,1)}, f32[1,1]{1,0:T(1,128)}) custom-call(f32[4,1024,128]{2,1,0:T(8,128)S(1)} %get-tuple-element.11.back_ref, f32[4,16,8,1024]{3,2,1,0:T(8,128)S(1)} %get-tuple-element.12.lat_ref, f32[4,16,8,1024]{3,2,1,0:T(8,128)S(1)} %get-tuple-element.13.lon_ref, ...), custom_call_target="tpu_custom_call" | custom-call | tf_op jit(solution)/shard_map/pallas_call | solution.py:474
